TPU v7x, 32 devices: a whole 2x2x4 slice. The times are simulated.
32 devices in a mesh: groups: 2 (over y), row: 4 (over z), col: 4 (over x, core).
Axes of the slice: x: 2, y: 2, z: 4, core: 2. Of those that a mesh axis runs over, the one named last changes fastest.
Arguments:
- raw_files: bfloat16 [128, 4, 8, 12000], P(('groups', 'row'), 'col'), parts along dimension 0
- file_channels: int32 [128, 4], P(('groups', 'row'), 'col'), parts along dimension 0, may hold values from 0 to 255, as said below
- reader_counts: int32 [8, 4], P(('groups', 'row'), 'col'), parts along dimension 0, may hold values from 0 to 16, as said below
- fir_taps: float32 [32], replicated, may hold values from -1 to 1
- band_bins: int32 [64], replicated, may hold values from 1 to 1499, as said below
Outputs:
- stack: bfloat16 [512, 4, 64, 128], P(('groups', 'row'), 'col'), parts along dimension 0
There are 2 independent parts, one for each index of `groups`. A program takes and returns all parts, laid end to end along the dimension named above; an argument that names none is the same for every part. Nothing has to cross between parts.
Inputs may be any that keep to these rules, and one draw needn't show every extreme that they name: `file_channels`: channel q belongs to owner row q // 64, column (q // 16) % 4. Every channel stands in exactly one live slot (slot below its reader's count), of a reader in its owner's column. Live slots of one reader name at most 4 channels of one owner; in every column some reader holds exactly 4 channels of every owner. Slots at or above the count hold arbitrary channel numbers. `reader_counts`: in every column some reader holds 16 live slots. `band_bins`: Distinct.
All inputs are finite; a program needn't handle non-finite values.
Results may differ from a plain program's by a relative error of at most 0.017.
Values may be sent and summed in bfloat16 or wider, within the bound.
No kernel may reach another device: no remote copies, remote signals or barrier semaphores. Data moves between devices by JAX's collectives and lax.ppermute only.
A program may use at most 64 MiB of HBM per device.

v0:
```python
import math
import jax
import jax.numpy as jnp
from jax import lax
from jax.sharding import PartitionSpec as P

CH_DEV = 16
DEC = 4


def decimate(signal, fir_taps):
    count, records, samples = signal.shape
    length = samples // DEC
    taps = fir_taps.shape[0]
    outputs = 128
    span = outputs * DEC
    blocks = (length + outputs - 1) // outputs
    total = (blocks + 1) * span
    padded = jnp.pad(signal, ((0, 0), (0, 0), (0, total - samples)))
    leading = padded[:, :, : blocks * span].reshape(count, records, blocks, span)
    following = padded[:, :, span:].reshape(count, records, blocks, span)[:, :, :, : taps - DEC]
    window = jnp.concatenate([leading, following], axis=3)
    positions = jnp.arange(span + taps - DEC, dtype=jnp.int32)[:, None]
    columns = jnp.arange(outputs, dtype=jnp.int32)[None, :]
    offset = positions - DEC * columns
    banded = jnp.zeros((span + taps - DEC, outputs), jnp.float32)
    for index in range(taps):
        banded = banded + jnp.where(offset == index, fir_taps[index], jnp.float32(0.0))
    upper = banded.astype(jnp.bfloat16)
    lower = (banded - upper.astype(jnp.float32)).astype(jnp.bfloat16)
    result = jnp.einsum("iqbw,wn->iqbn", window, upper, preferred_element_type=jnp.float32)
    result = result + jnp.einsum("iqbw,wn->iqbn", window, lower, preferred_element_type=jnp.float32)
    return result.reshape(count, records, blocks * outputs)[:, :, :length].astype(jnp.bfloat16)


def whiten(signal, fir_taps, band_bins):
    count, records, samples = signal.shape
    length = samples // DEC
    decimated = decimate(signal, fir_taps)
    steps = jnp.arange(length, dtype=jnp.int32)
    product = band_bins[None, :] * steps[:, None] % length
    angle = 2.0 * math.pi / length * product.astype(jnp.float32)
    table = jnp.concatenate([jnp.cos(angle), -jnp.sin(angle)], axis=1).astype(jnp.bfloat16)
    spectra = jnp.dot(
        decimated.reshape(count * records, length), table, preferred_element_type=jnp.float32
    )
    power = jnp.mean(spectra * spectra, axis=1, keepdims=True)
    white = spectra / jnp.sqrt(power + 1e-06)
    return white.reshape(count, records, table.shape[1]).astype(jnp.bfloat16)


def slot_plan(file_channels, reader_counts, nrows, ncols, capacity):
    channels = file_channels[:, 0]
    slots = channels.shape[0]
    order = jnp.arange(slots, dtype=jnp.int32)
    live = order < reader_counts[0, 0]
    owner = channels // (CH_DEV * ncols)
    place = channels % CH_DEV
    earlier = (owner[None, :] == owner[:, None]) & live[None, :] & (order[None, :] < order[:, None])
    rank = jnp.sum(earlier.astype(jnp.int32), axis=1)
    where_to = jnp.where(live, owner * capacity + rank, -1)
    target = jnp.arange(nrows * capacity, dtype=jnp.int32)
    match = (where_to[None, :] == target[:, None]).astype(jnp.int32)
    filled = jnp.sum(match, axis=1) > 0
    source = jnp.sum(match * order[None, :], axis=1)
    label = jnp.where(filled, jnp.sum(match * place[None, :], axis=1), -1)
    return (source, filled, label)


def pack(data, source, filled, nrows, capacity):
    chosen = jnp.where(filled[:, None, None], data[source], jnp.zeros((), data.dtype))
    return chosen.reshape((nrows, capacity) + data.shape[1:])


def settle(received, labels):
    flat = received.reshape((-1,) + received.shape[2:])
    marks = labels.reshape(-1).astype(jnp.int32)
    total = marks.shape[0]
    match = (marks[None, :] == jnp.arange(CH_DEV, dtype=jnp.int32)[:, None]).astype(jnp.int32)
    source = jnp.sum(match * jnp.arange(total, dtype=jnp.int32)[None, :], axis=1)
    return flat[source]


def on_device(raw_files, file_channels, reader_counts, fir_taps, band_bins):
    nrows = lax.axis_size("row")
    ncols = lax.axis_size("col")
    capacity = max(2, (CH_DEV + nrows - 1) // nrows)
    source, filled, label = slot_plan(file_channels, reader_counts, nrows, ncols, capacity)
    labels = label.reshape(nrows, capacity).astype(jnp.bfloat16)
    reader_white = whiten(raw_files[:, 0], fir_taps, band_bins)
    outgoing = pack(reader_white, source, filled, nrows, capacity)
    arrived, arrived_labels = (
        lax.all_to_all(outgoing, "row", split_axis=0, concat_axis=0, tiled=True),
        lax.all_to_all(labels, "row", split_axis=0, concat_axis=0, tiled=True),
    )
    white_own = settle(arrived, arrived_labels)
    records = white_own.shape[1]
    width = white_own.shape[2] // 2
    row_white = lax.all_gather(white_own, "col", axis=0, tiled=True)
    left_count = row_white.shape[0]
    left = (
        row_white.reshape(left_count, records, 2, width)
        .transpose(0, 2, 1, 3)
        .reshape(left_count, 2 * records, width)
    )
    piece = lax.all_gather(white_own, "row", axis=0, tiled=True)
    right_count = piece.shape[0]
    split_piece = piece.reshape(right_count, records, 2, width)
    piece_re = split_piece[:, :, 0, :]
    piece_im = split_piece[:, :, 1, :]
    right_real = jnp.concatenate([piece_re, piece_im], axis=1)
    right_imag = jnp.concatenate([-piece_im, piece_re], axis=1)
    real = jnp.einsum("ikb,jkb->ijb", left, right_real, preferred_element_type=jnp.float32)
    imag = jnp.einsum("ikb,jkb->ijb", left, right_imag, preferred_element_type=jnp.float32)
    stacked = (jnp.concatenate([real, imag], axis=2) / records).astype(jnp.bfloat16)
    return stacked[:, None, :, :]


def solution(mesh):
    return jax.shard_map(
        on_device,
        mesh=mesh,
        in_specs=(
            P(("groups", "row"), "col", None, None),
            P(("groups", "row"), "col"),
            P(("groups", "row"), "col"),
            P(),
            P(),
        ),
        out_specs=P(("groups", "row"), "col", None, None),
        check_vma=False,
    )
```

profile of v0, /device:TPU:0, one launch (start us, length us, event | category | flops | bytes accessed | tf_op | source)
XLA Modules:
  0.0 111.3 jit_solution(5888975628344206008)
XLA Ops:
  0.0 0.7 and_select_fusion.2
  0.7 0.7 fusion.64
  2.0 0.2 convert_reduce_fusion.1
  2.2 0.1 select_reduce_fusion.1
  2.3 0.7 convert_element_type.76
  3.0 6.3 %all-to-all-start.1 = ((bf16[4,1,4]{2,1,0:T(2,128)(2,1)}), bf16[4,1,4]{2,1,0:T(2,128)(2,1)S(1)}, u32[]{:S(2)}, u32[]{:S(2)}) async-start(bf16[4,1,4]{2,1,0:T(2,128)(2,1)} %convert_element_type.76), calls=%async_computation.1 | async-start | bytes 4096 | tf_op jit(solution)/shard_map/all_to_all | solution.py:94
  9.4 2.1 %fusion.137 = (f32[1]{0:T(128)}, f32[1]{0:T(128)}, f32[1]{0:T(128)}, f32[1]{0:T(128)}, f32[1]{0:T(128)}, /*index=5*/f32[1]{0:T(128)}, f32[1]{0:T(128)}, f32[1]{0...) fusion(f32[32]{0:T(128)} %param.8), kind=kLoop, calls=%fused_computation.186 | loop fusion | bytes 152 | tf_op jit(solution)/shard_map/slice | solution.py:28
  11.5 1.8 %fusion.138 = (f32[1]{0:T(128)}, f32[1]{0:T(128)}, f32[1]{0:T(128)}, f32[1]{0:T(128)}, f32[1]{0:T(128)}, /*index=5*/f32[1]{0:T(128)}, f32[1]{0:T(128)}, f32[1]{0...) fusion(f32[32]{0:T(128)} %param.8), kind=kLoop, calls=%fused_computation.187 | loop fusion | bytes 104 | tf_op jit(solution)/shard_map/slice | solution.py:28
  13.3 3.2 %pad_slice_fusion.1 = (bf16[16,8,12288]{2,1,0:T(8,128)(2,1)S(1)}, bf16[16,8,12288]{2,1,0:T(8,128)(2,1)S(1)}) fusion(bf16[16,8,12000]{2,1,0:T(8,128)(2,1)} %bitcast.115), kind=kLoop, calls=%fused_computation.6 | loop fusion | bytes 9363456 | tf_op jit(solution)/shard_map/slice | solution.py:20
  16.5 1.3 %copy.29 = bf16[16,8,24,512]{3,2,1,0:T(8,128)(2,1)S(1)} copy(bf16[16,8,24,512]{3,1,2,0:T(8,128)(2,1)S(1)} %bitcast.112) | data formatting | bytes 6291456
  17.8 0.1 slice.157
  17.9 1.3 %copy.30 = bf16[16,8,24,512]{3,2,1,0:T(8,128)(2,1)S(1)} copy(bf16[16,8,24,512]{3,1,2,0:T(8,128)(2,1)S(1)} %bitcast.111) | data formatting | bytes 6291456
  19.2 22.2 %fusion = f32[16,8,24,128]{3,2,1,0:T(8,128)S(1)} fusion(bf16[16,8,24,28]{3,2,1,0:T(8,128)(2,1)S(1)} %slice.157, bf16[16,8,24,512]{3,2,1,0:T(8,128)(2,1)S(1)} %copy.30, f32[]{:T(128)} %bitcast.35, f32[]{:T(128)} %bitcast.34, f32[]{:T(128)} %bitcast.33, f32[]{:T(128)} %bitcast.32, f32[]{:T(128)} %bitcast.31, f32[]{:T(128)} %bitcast.30, f32[]{:T(128)} %bitcast.29, ...), kind=kOutput, calls=%fused_computation.7 | convolution fusion | flops 438220800 | bytes 4891264 | tf_op jit(solution)/shard_map/iqbw,wn->iqbn/dot_general | solution.py:32
  41.4 22.0 %add_convert_fusion = bf16[16,8,24,128]{3,2,1,0:T(8,128)(2,1)S(1)} fusion(f32[16,8,24,128]{3,2,1,0:T(8,128)S(1)} %fusion, bf16[16,8,24,28]{3,2,1,0:T(8,128)(2,1)S(1)} %slice.157, bf16[16,8,24,512]{3,2,1,0:T(8,128)(2,1)S(1)} %copy.30, f32[]{:T(128)} %bitcast.35, f32[]{:T(128)} %bitcast.34, f32[]{:T(128)} %bitcast.33, f32[]{:T(128)} %bitcast.32, ...), kind=kOutput, calls=%fused_computation.11 | convolution fusion | flops 438799872 | bytes 5677696 | tf_op jit(solution)/shard_map/iqbw,wn->iqbn/dot_general | solution.py:31
  63.4 0.3 reshape.222
  63.8 3.6 %cosine_convert_fusion = (bf16[3000,64]{0,1:T(8,128)(2,1)S(1)}, bf16[3000,64]{0,1:T(8,128)(2,1)S(1)}) fusion(s32[64]{0:T(128)S(1)} %copy-done), kind=kLoop, calls=%fused_computation.21 | loop fusion | flops 2304000 | bytes 768256 | tf_op jit(solution)/shard_map/convert.1
  67.4 0.5 multiply_reduce_fusion
  68.0 0.6 gather_fusion
  68.6 0.7 broadcast_select_fusion
  69.3 5.1 %all-to-all-start = ((bf16[4,4,8,128]{3,2,1,0:T(8,128)(2,1)}), bf16[4,4,8,128]{3,2,1,0:T(8,128)(2,1)S(1)}, u32[]{:S(2)}, u32[]{:S(2)}) async-start(bf16[4,4,8,128]{3,2,1,0:T(8,128)(2,1)} %broadcast_select_fusion), calls=%async_computation | async-start | bytes 65536 | tf_op jit(solution)/shard_map/all_to_all | solution.py:93
  74.7 5.4 %all-to-all-done = bf16[4,4,8,128]{3,2,1,0:T(8,128)(2,1)S(1)} async-done(((bf16[4,4,8,128]{3,2,1,0:T(8,128)(2,1)}), bf16[4,4,8,128]{3,2,1,0:T(8,128)(2,1)S(1)}, u32[]{:S(2)}, u32[]{:S(2)}) %all-to-all-start) | async-done | bytes 32800 | tf_op jit(solution)/shard_map/all_to_all | solution.py:93
  80.1 0.6 gather_fusion.1
  80.6 13.3 %all-gather = bf16[64,8,128]{2,1,0:T(8,128)(2,1)S(1)} all-gather(bf16[16,8,128]{2,1,0:T(8,128)(2,1)S(1)} %gather_fusion.1), channel_id=2, replica_groups=mesh['groups'=2,'row'=4,'col'=4] {'row'}, dimensions={0}, use_global_device_ids=true | all-gather | bytes 163840 | tf_op jit(solution)/shard_map/all_gather | solution.py:106
  94.0 5.6 %all-gather.1 = bf16[64,8,128]{2,1,0:T(8,128)(2,1)S(1)} all-gather(bf16[16,8,128]{2,1,0:T(8,128)(2,1)S(1)} %gather_fusion.1), channel_id=3, replica_groups=mesh['groups'=2,'row'=4,'col'=4] {'col'}, dimensions={0}, use_global_device_ids=true | all-gather | bytes 163840 | tf_op jit(solution)/shard_map/all_gather | solution.py:99
  99.6 0.2 copy.19
  99.8 0.1 reshape.226
  100.0 0.4 copy.20
  100.4 0.5 fusion.44
  100.8 3.1 %copy.21 = f32[64,64,64]{0,1,2:T(8,128)} copy(f32[64,64,64]{2,1,0:T(8,128)S(1)} %fusion.44) | data formatting | bytes 2097152 | tf_op jit(solution)/shard_map/ikb,jkb->ijb/dot_general | solution.py:113
  103.9 0.5 fusion.48
  104.4 3.1 %copy.22 = f32[64,64,64]{0,1,2:T(8,128)} copy(f32[64,64,64]{2,1,0:T(8,128)S(1)} %fusion.48) | data formatting | bytes 2097152 | tf_op jit(solution)/shard_map/ikb,jkb->ijb/dot_general | solution.py:114
  107.5 3.8 %fusion.2 = bf16[64,1,64,128]{3,2,1,0:T(8,128)(2,1)} fusion(f32[64,1,64,64]{3,2,1,0:T(8,128)} %bitcast.114, f32[64,1,64,64]{3,2,1,0:T(8,128)} %bitcast.113), kind=kLoop, calls=%fused_computation.10 | loop fusion | flops 1572864 | bytes 3145728 | tf_op jit(solution)/shard_map/convert_element_type | solution.py:115
  (20 shorter events, 0.5 us)
Async XLA Ops:
  3.0 66.3 %all-to-all-start.1 = ((bf16[4,1,4]{2,1,0:T(2,128)(2,1)}), bf16[4,1,4]{2,1,0:T(2,128)(2,1)S(1)}, u32[]{:S(2)}, u32[]{:S(2)}) async-start(bf16[4,1,4]{2,1,0:T(2,128)(2,1)} %convert_element_type.76), calls=%async_computation.1 | async-start | bytes 4096 | tf_op jit(solution)/shard_map/all_to_all | solution.py:94
  41.4 22.4 %copy-start = (s32[64]{0:T(128)S(1)}, s32[64]{0:T(128)}, u32[]{:S(2)}) copy-start(s32[64]{0:T(128)} %param.9) | copy-start | bytes 772
  69.3 10.8 %all-to-all-start = ((bf16[4,4,8,128]{3,2,1,0:T(8,128)(2,1)}), bf16[4,4,8,128]{3,2,1,0:T(8,128)(2,1)S(1)}, u32[]{:S(2)}, u32[]{:S(2)}) async-start(bf16[4,4,8,128]{3,2,1,0:T(8,128)(2,1)} %broadcast_select_fusion), calls=%async_computation | async-start | bytes 65536 | tf_op jit(solution)/shard_map/all_to_all | solution.py:93
where the time goes:
time: 112 us; the launch traced here: 111 us
  matrix products  45.6 us (41%)
  local copies, waits for them, and re-layouts  19 us (17%)
  blocking collectives  18.9 us (17%)
  starting transfers between devices  11.4 us (10%)
  other arithmetic  10.1 us (9%)
  waiting for transfers between devices  5.41 us (5%)
    dot_general x1, matrix products, decimate(): jnp.einsum('iqbw,wn->iqbn', window, lower, preferred_element_type=jnp.flo...  22.2 us
    dot_general x1, matrix products, decimate(): jnp.einsum('iqbw,wn->iqbn', window, upper, preferred_element_type=jnp.flo...  22 us
    all_gather x1, blocking collectives, on_device(): piece = lax.all_gather(white_own, 'row', axis=0, tiled=True)  13.3 us
    all_to_all x1, starting transfers between devices, on_device(): lax.all_to_all(labels, 'row', split_axis=0, concat_axis=0, tiled=True)  6.35 us
    all_gather x1, blocking collectives, on_device(): row_white = lax.all_gather(white_own, 'col', axis=0, tiled=True)  5.58 us
    all_to_all x1, waiting for transfers between devices, on_device(): lax.all_to_all(outgoing, 'row', split_axis=0, concat_axis=0, tiled=True)  5.41 us
    all_to_all x1, starting transfers between devices, on_device(): lax.all_to_all(outgoing, 'row', split_axis=0, concat_axis=0, tiled=True)  5.09 us
    slice x2, local copies, waits for them, and re-layouts, decimate(): fir_taps[index]  3.9 us
  transfers between devices with their start and end apart: 2, of which 1 were waited for; matrix products, arithmetic and copies ran while one was open for 54% of the time, Pallas kernels for 0%

commit v1 on v0

--- a/solution.py
+++ b/solution.py
@@ -6,6 +6,28 @@
 
 CH_DEV = 16
 DEC = 4
+
+
+def in_blocks(array, dim, length):
+    before, after = (array.shape[:dim], array.shape[dim + 1 :])
+    return jnp.moveaxis(array.reshape(*before, length, -1, *after), dim, 0)
+
+
+def in_order(pieces, dim):
+    lengths = list(pieces.shape[1:])
+    lengths[dim] *= pieces.shape[0]
+    return jnp.moveaxis(pieces, 0, dim).reshape(lengths)
+
+
+def swapped_with_each(x, axis, split_dim, concat_dim):
+    peers, here = (lax.axis_size(axis), lax.axis_index(axis))
+    blocks = in_blocks(x, split_dim, peers)
+    outs = [blocks[here]]
+    for step in range(1, peers):
+        sent = blocks[here ^ step]
+        outs.append(lax.ppermute(sent, axis, [(i, i ^ step) for i in range(peers)]))
+    blocks = jnp.stack(outs)[here ^ jnp.arange(peers)]
+    return in_order(blocks, concat_dim)
 
 
 def decimate(signal, fir_taps):
@@ -91,7 +113,7 @@
     outgoing = pack(reader_white, source, filled, nrows, capacity)
     arrived, arrived_labels = (
         lax.all_to_all(outgoing, "row", split_axis=0, concat_axis=0, tiled=True),
-        lax.all_to_all(labels, "row", split_axis=0, concat_axis=0, tiled=True),
+        swapped_with_each(labels, "row", 0, 0),
     )
     white_own = settle(arrived, arrived_labels)
     records = white_own.shape[1]

time: 112 us -> 112 us (level)
    all_to_all x1 -> x0, starting transfers between devices: 6.35 us -> none  [on_device(): lax.all_to_all(labels, 'row', split_axis=0, concat_axis=0, tiled=True)]
    all_to_all x1, waiting for transfers between devices: 5.41 us -> 0.01 us  [on_device(): lax.all_to_all(outgoing, 'row', split_axis=0, concat_axis=0, tiled=True)]
    ppermute x0 -> x3, waiting for transfers between devices: none -> 5.27 us  [swapped_with_each(): outs.append(lax.ppermute(sent, axis, [(i, i ^ step) for i in range(peers)]))]
    ppermute x0 -> x3, starting transfers between devices: none -> 4.53 us  [swapped_with_each(): outs.append(lax.ppermute(sent, axis, [(i, i ^ step) for i in range(peers)]))]
    all_to_all x1, starting transfers between devices: 5.09 us -> 6.35 us  [on_device(): lax.all_to_all(outgoing, 'row', split_axis=0, concat_axis=0, tiled=True)]
    another operation x1 -> x2, other arithmetic: 3.59 us -> 3.6 us
    unnamed x4 -> x5, local copies, waits for them, and re-layouts: 2.56 us -> 2.56 us
  transfers between devices with their start and end apart: 2 -> 4, of which waited for: 1 -> 2; matrix products, arithmetic and copies ran while one was open for 54% -> 1% of each run, Pallas kernels for 0% -> 0%
where the time goes in v1:
time: 112 us; the launch traced here: 111 us
  matrix products  45.8 us (41%)
  local copies, waits for them, and re-layouts  19 us (17%)
  blocking collectives  19 us (17%)
  starting transfers between devices  10.9 us (10%)
  other arithmetic  10.1 us (9%)
  waiting for transfers between devices  5.27 us (5%)
    dot_general x1, matrix products, decimate(): jnp.einsum('iqbw,wn->iqbn', window, lower, preferred_element_type=jnp.flo...  22.3 us
    dot_general x1, matrix products, decimate(): jnp.einsum('iqbw,wn->iqbn', window, upper, preferred_element_type=jnp.flo...  22.1 us
    all_gather x1, blocking collectives, on_device(): piece = lax.all_gather(white_own, 'row', axis=0, tiled=True)  13.4 us
    all_to_all x1, starting transfers between devices, on_device(): lax.all_to_all(outgoing, 'row', split_axis=0, concat_axis=0, tiled=True)  6.35 us
    all_gather x1, blocking collectives, on_device(): row_white = lax.all_gather(white_own, 'col', axis=0, tiled=True)  5.58 us
    ppermute x3, waiting for transfers between devices, swapped_with_each(): outs.append(lax.ppermute(sent, axis, [(i, i ^ step) for i in range(peers)]))  5.27 us
    ppermute x3, starting transfers between devices, swapped_with_each(): outs.append(lax.ppermute(sent, axis, [(i, i ^ step) for i in range(peers)]))  4.53 us
    slice x2, local copies, waits for them, and re-layouts, decimate(): fir_taps[index]  3.91 us
  transfers between devices with their start and end apart: 4, of which 2 were waited for; matrix products, arithmetic and copies ran while one was open for 1% of the time, Pallas kernels for 0%

profile of v1, /device:TPU:0, one launch (start us, length us, event | category | flops | bytes accessed | tf_op | source)
XLA Modules:
  0.0 110.9 jit_solution(12567943602557087947)
XLA Ops:
  0.0 2.1 %fusion.139 = (f32[1]{0:T(128)}, f32[1]{0:T(128)}, f32[1]{0:T(128)}, f32[1]{0:T(128)}, f32[1]{0:T(128)}, /*index=5*/f32[1]{0:T(128)}, f32[1]{0:T(128)}, f32[1]{0...) fusion(f32[32]{0:T(128)} %param.8), kind=kLoop, calls=%fused_computation.196 | loop fusion | bytes 152 | tf_op jit(solution)/shard_map/slice | solution.py:50
  2.1 1.8 %fusion.140 = (f32[1]{0:T(128)}, f32[1]{0:T(128)}, f32[1]{0:T(128)}, f32[1]{0:T(128)}, f32[1]{0:T(128)}, /*index=5*/f32[1]{0:T(128)}, f32[1]{0:T(128)}, f32[1]{0...) fusion(f32[32]{0:T(128)} %param.8), kind=kLoop, calls=%fused_computation.197 | loop fusion | bytes 104 | tf_op jit(solution)/shard_map/slice | solution.py:50
  3.9 0.7 and_select_fusion.2
  4.6 0.7 fusion.68
  5.3 3.2 %pad_slice_fusion.1 = (bf16[16,8,12288]{2,1,0:T(8,128)(2,1)S(1)}, bf16[16,8,12288]{2,1,0:T(8,128)(2,1)S(1)}) fusion(bf16[16,8,12000]{2,1,0:T(8,128)(2,1)} %bitcast.125), kind=kLoop, calls=%fused_computation.7 | loop fusion | bytes 9363456 | tf_op jit(solution)/shard_map/slice | solution.py:42
  8.5 1.3 %copy.28 = bf16[16,8,24,512]{3,2,1,0:T(8,128)(2,1)S(1)} copy(bf16[16,8,24,512]{3,1,2,0:T(8,128)(2,1)S(1)} %bitcast.122) | data formatting | bytes 6291456
  9.9 1.3 %copy.29 = bf16[16,8,24,512]{3,2,1,0:T(8,128)(2,1)S(1)} copy(bf16[16,8,24,512]{3,1,2,0:T(8,128)(2,1)S(1)} %bitcast.121) | data formatting | bytes 6291456
  11.2 22.3 %fusion = f32[16,8,24,128]{3,2,1,0:T(8,128)S(1)} fusion(bf16[16,8,24,28]{3,2,1,0:T(8,128)(2,1)S(1)} %slice.159, bf16[16,8,24,512]{3,2,1,0:T(8,128)(2,1)S(1)} %copy.29, f32[]{:T(128)} %bitcast.35, f32[]{:T(128)} %bitcast.34, f32[]{:T(128)} %bitcast.33, f32[]{:T(128)} %bitcast.32, f32[]{:T(128)} %bitcast.31, f32[]{:T(128)} %bitcast.30, f32[]{:T(128)} %bitcast.29, ...), kind=kOutput, calls=%fused_computation.8 | convolution fusion | flops 438220800 | bytes 4891264 | tf_op jit(solution)/shard_map/iqbw,wn->iqbn/dot_general | solution.py:54
  33.4 22.1 %add_convert_fusion = bf16[16,8,24,128]{3,2,1,0:T(8,128)(2,1)S(1)} fusion(f32[16,8,24,128]{3,2,1,0:T(8,128)S(1)} %fusion, bf16[16,8,24,28]{3,2,1,0:T(8,128)(2,1)S(1)} %slice.159, bf16[16,8,24,512]{3,2,1,0:T(8,128)(2,1)S(1)} %copy.29, f32[]{:T(128)} %bitcast.35, f32[]{:T(128)} %bitcast.34, f32[]{:T(128)} %bitcast.33, f32[]{:T(128)} %bitcast.32, ...), kind=kOutput, calls=%fused_computation.12 | convolution fusion | flops 438799872 | bytes 5677696 | tf_op jit(solution)/shard_map/iqbw,wn->iqbn/dot_general | solution.py:53
  55.5 0.3 reshape.214
  55.9 3.6 %cosine_convert_fusion = (bf16[3000,64]{0,1:T(8,128)(2,1)S(1)}, bf16[3000,64]{0,1:T(8,128)(2,1)S(1)}) fusion(s32[64]{0:T(128)S(1)} %copy-done), kind=kLoop, calls=%fused_computation.22 | loop fusion | flops 2304000 | bytes 768256 | tf_op jit(solution)/shard_map/convert.1
  59.5 0.5 multiply_reduce_fusion
  60.6 0.2 convert_reduce_fusion.1
  60.8 0.1 select_reduce_fusion.1
  61.2 0.6 gather_fusion
  61.7 0.7 broadcast_select_fusion
  62.5 6.4 %all-to-all-start = ((bf16[4,4,8,128]{3,2,1,0:T(8,128)(2,1)}), bf16[4,4,8,128]{3,2,1,0:T(8,128)(2,1)S(1)}, u32[]{:S(2)}, u32[]{:S(2)}) async-start(bf16[4,4,8,128]{3,2,1,0:T(8,128)(2,1)} %broadcast_select_fusion), calls=%async_computation | async-start | bytes 65536 | tf_op jit(solution)/shard_map/all_to_all | solution.py:115
  68.9 2.1 %collective-permute-start = (bf16[1,4]{1,0:T(2,128)(2,1)S(1)}, bf16[1,4]{1,0:T(2,128)(2,1)S(1)}, u32[]{:S(2)}, u32[]{:S(2)}) collective-permute-start(bf16[1,4]{1,0:T(2,128)(2,1)S(1)} %get-tuple-element.15), channel_id=1, source_target_pairs={{0,4},{4,0},{8,12},{12,8},{1,5},{5,1},{9,13},{13,9},{2,6},{6,2},{1... | collective-permute-start | bytes 32 | tf_op jit(solution)/shard_map/ppermute | solution.py:28
  71.0 2.4 %collective-permute-start.1 = (bf16[1,4]{1,0:T(2,128)(2,1)S(1)}, bf16[1,4]{1,0:T(2,128)(2,1)S(1)}, u32[]{:S(2)}, u32[]{:S(2)}) collective-permute-start(bf16[1,4]{1,0:T(2,128)(2,1)S(1)} %get-tuple-element.14), channel_id=1, source_target_pairs={{0,8},{4,12},{8,0},{12,4},{1,9},{5,13},{9,1},{13,5},{2,10},{6,14},... | collective-permute-start | bytes 32 | tf_op jit(solution)/shard_map/ppermute | solution.py:28
  73.5 2.0 %collective-permute-done.1 = bf16[1,4]{1,0:T(2,128)(2,1)S(1)} collective-permute-done((bf16[1,4]{1,0:T(2,128)(2,1)S(1)}, bf16[1,4]{1,0:T(2,128)(2,1)S(1)}, u32[]{:S(2)}, u32[]{:S(2)}) %collective-permute-start.1) | collective-permute-done | bytes 40 | tf_op jit(solution)/shard_map/ppermute | solution.py:28
  75.5 3.3 %collective-permute-done.2 = bf16[1,4]{1,0:T(2,128)(2,1)S(1)} collective-permute-done((bf16[1,4]{1,0:T(2,128)(2,1)S(1)}, bf16[1,4]{1,0:T(2,128)(2,1)S(1)}, u32[]{:S(2)}, u32[]{:S(2)}) %collective-permute-start.2) | collective-permute-done | bytes 40 | tf_op jit(solution)/shard_map/ppermute | solution.py:28
  78.8 0.6 gather_fusion.1
  79.6 0.6 gather_fusion.2
  80.1 13.4 %all-gather = bf16[64,8,128]{2,1,0:T(8,128)(2,1)S(1)} all-gather(bf16[16,8,128]{2,1,0:T(8,128)(2,1)S(1)} %gather_fusion.2), channel_id=2, replica_groups=mesh['groups'=2,'row'=4,'col'=4] {'row'}, dimensions={0}, use_global_device_ids=true | all-gather | bytes 163840 | tf_op jit(solution)/shard_map/all_gather | solution.py:128
  93.6 5.6 %all-gather.1 = bf16[64,8,128]{2,1,0:T(8,128)(2,1)S(1)} all-gather(bf16[16,8,128]{2,1,0:T(8,128)(2,1)S(1)} %gather_fusion.2), channel_id=3, replica_groups=mesh['groups'=2,'row'=4,'col'=4] {'col'}, dimensions={0}, use_global_device_ids=true | all-gather | bytes 163840 | tf_op jit(solution)/shard_map/all_gather | solution.py:121
  99.2 0.2 copy.16
  99.6 0.4 copy.17
  100.0 0.5 fusion.44
  100.4 3.1 %copy.18 = f32[64,64,64]{0,1,2:T(8,128)} copy(f32[64,64,64]{2,1,0:T(8,128)S(1)} %fusion.44) | data formatting | bytes 2097152 | tf_op jit(solution)/shard_map/ikb,jkb->ijb/dot_general | solution.py:135
  103.5 0.5 fusion.48
  104.0 3.1 %copy.19 = f32[64,64,64]{0,1,2:T(8,128)} copy(f32[64,64,64]{2,1,0:T(8,128)S(1)} %fusion.48) | data formatting | bytes 2097152 | tf_op jit(solution)/shard_map/ikb,jkb->ijb/dot_general | solution.py:136
  107.1 3.8 %fusion.2 = bf16[64,1,64,128]{3,2,1,0:T(8,128)(2,1)} fusion(f32[64,1,64,64]{3,2,1,0:T(8,128)} %bitcast.124, f32[64,1,64,64]{3,2,1,0:T(8,128)} %bitcast.123), kind=kLoop, calls=%fused_computation.11 | loop fusion | flops 1572864 | bytes 3145728 | tf_op jit(solution)/shard_map/convert_element_type | solution.py:137
  (30 shorter events, 1.0 us)
Async XLA Ops:
  33.4 22.4 %copy-start = (s32[64]{0:T(128)S(1)}, s32[64]{0:T(128)}, u32[]{:S(2)}) copy-start(s32[64]{0:T(128)} %param.9) | copy-start | bytes 772
  62.5 17.1 %all-to-all-start = ((bf16[4,4,8,128]{3,2,1,0:T(8,128)(2,1)}), bf16[4,4,8,128]{3,2,1,0:T(8,128)(2,1)S(1)}, u32[]{:S(2)}, u32[]{:S(2)}) async-start(bf16[4,4,8,128]{3,2,1,0:T(8,128)(2,1)} %broadcast_select_fusion), calls=%async_computation | async-start | bytes 65536 | tf_op jit(solution)/shard_map/all_to_all | solution.py:115
  68.9 4.5 %collective-permute-start = (bf16[1,4]{1,0:T(2,128)(2,1)S(1)}, bf16[1,4]{1,0:T(2,128)(2,1)S(1)}, u32[]{:S(2)}, u32[]{:S(2)}) collective-permute-start(bf16[1,4]{1,0:T(2,128)(2,1)S(1)} %get-tuple-element.15), channel_id=1, source_target_pairs={{0,4},{4,0},{8,12},{12,8},{1,5},{5,1},{9,13},{13,9},{2,6},{6,2},{1... | collective-permute-start | bytes 32 | tf_op jit(solution)/shard_map/ppermute | solution.py:28
  71.0 4.5 %collective-permute-start.1 = (bf16[1,4]{1,0:T(2,128)(2,1)S(1)}, bf16[1,4]{1,0:T(2,128)(2,1)S(1)}, u32[]{:S(2)}, u32[]{:S(2)}) collective-permute-start(bf16[1,4]{1,0:T(2,128)(2,1)S(1)} %get-tuple-element.14), channel_id=1, source_target_pairs={{0,8},{4,12},{8,0},{12,4},{1,9},{5,13},{9,1},{13,5},{2,10},{6,14},... | collective-permute-start | bytes 32 | tf_op jit(solution)/shard_map/ppermute | solution.py:28
  73.4 5.4 %collective-permute-start.2 = (bf16[1,4]{1,0:T(2,128)(2,1)S(1)}, bf16[1,4]{1,0:T(2,128)(2,1)S(1)}, u32[]{:S(2)}, u32[]{:S(2)}) collective-permute-start(bf16[1,4]{1,0:T(2,128)(2,1)S(1)} %get-tuple-element.13), channel_id=1, source_target_pairs={{0,12},{4,8},{8,4},{12,0},{1,13},{5,9},{9,5},{13,1},{2,14},{6,10},... | collective-permute-start | bytes 32 | tf_op jit(solution)/shard_map/ppermute | solution.py:28
